TPU v7x, 32 devices: a whole 2x2x4 slice. The times are simulated.
32 devices in a mesh: grp: 2 (over x), row: 16 (over z, y, core).
Axes of the slice: x: 2, y: 2, z: 4, core: 2. Of those that a mesh axis runs over, the one named last changes fastest.
Arguments:
- slc: bfloat16 [2, 300, 64, 256], P(None, None, ('grp', 'row')), parts along dimension 2, may hold values from -8 to 8
- mask: int32 [25, 64, 256], P(None, ('grp', 'row')), parts along dimension 1, may hold values 0 or 1
- ref_index: int32 [2], P('grp'), parts along dimension 0, may hold values from 0 to 8191
Outputs:
- linked: float32 [2, 300, 64, 256], P(None, None, ('grp', 'row')), parts along dimension 2
There are 2 independent parts, one for each index of `grp`. A program takes and returns all parts, laid end to end along the dimension named above; each array names one. Nothing has to cross between parts.
All inputs are finite; a program needn't handle non-finite values. No bound on the sum of `mask` on one device may be relied on, other than what follows from the above.
Results may differ from a plain program's by a relative error of at most 0.0046.
Values may be sent and summed in bfloat16 or wider, within the bound.
A program may use at most 64 MiB of HBM per device.

v0:
```python
import jax
import jax.numpy as jnp
from jax import lax
from jax.experimental import pallas as pl
from jax.experimental.pallas import tpu as pltpu
from jax.sharding import PartitionSpec as P

HALF = 2
ITERS = 2
WIDTH = 2 * HALF + 1
LANE = 128
SUB = 16
MESH = pl.DeviceIdType.MESH


def round_up(value, unit):
    return (value + unit - 1) // unit * unit


def row_of(column_sums):
    return jnp.sum(column_sums.T, axis=0, keepdims=True)


def kernel(
    n, ndate, total_rows, x_ref, mask_ref, index_ref, out_ref,
    low, high, flat, turned, weight, coef, column, powers, refs,
    low_sem, high_sem, power_sem, ref_sem,
):
    rows, depth, cols = x_ref.shape
    half_depth = depth // 2
    blocks = cols // LANE
    long_dates = powers.shape[2]
    long_depth = refs.shape[2]
    me = lax.axis_index("row")
    first_row = me * rows

    def peer(k):
        return lax.rem(me + k, n)

    barrier = pltpu.get_barrier_semaphore()

    @pl.loop(1, n)
    def _(k):
        pl.semaphore_signal(barrier, inc=1, device_id={"row": peer(k)}, device_id_type=MESH)

    column[...] = jnp.zeros_like(column)
    sums = jnp.zeros((half_depth, LANE), jnp.float32)
    for r in range(rows):
        for part in range(2):
            for block in range(blocks):
                piece = x_ref[r, part * half_depth:(part + 1) * half_depth, block * LANE:(block + 1) * LANE]
                piece = piece.astype(jnp.float32)
                sums = sums + piece * piece
    column[0:half_depth, :] = sums
    powers[me] = row_of(column[0:long_dates, :])

    pl.semaphore_wait(barrier, n - 1)

    def exchange(buffer, sems):
        def copy(k, slot):
            return pltpu.make_async_remote_copy(
                src_ref=buffer.at[slot], dst_ref=buffer.at[slot],
                send_sem=sems.at[0, k], recv_sem=sems.at[1, slot],
                device_id={"row": peer(k)}, device_id_type=MESH,
            )

        def start():
            @pl.loop(1, n)
            def _(k):
                copy(k, me).start()

        def finish():
            @pl.loop(1, n)
            def _(k):
                copy(k, peer(k)).wait_recv()

            @pl.loop(1, n)
            def _(k):
                copy(k, me).wait_send()

        return start, finish

    start_power, finish_power = exchange(powers, power_sem)
    start_ref, finish_ref = exchange(refs, ref_sem)
    start_power()

    up = pltpu.make_async_remote_copy(
        src_ref=x_ref.at[rows - HALF:rows], dst_ref=low, send_sem=low_sem.at[0], recv_sem=low_sem.at[1],
        device_id={"row": jnp.minimum(me + 1, n - 1)}, device_id_type=MESH,
    )
    down = pltpu.make_async_remote_copy(
        src_ref=x_ref.at[0:HALF], dst_ref=high, send_sem=high_sem.at[0], recv_sem=high_sem.at[1],
        device_id={"row": jnp.maximum(me - 1, 0)}, device_id_type=MESH,
    )
    has_next = me < n - 1
    has_prev = me > 0
    pl.when(has_next)(up.start)
    pl.when(has_prev)(down.start)

    @pl.when(me == 0)
    def _():
        low[...] = jnp.zeros_like(low)

    @pl.when(me == n - 1)
    def _():
        high[...] = jnp.zeros_like(high)

    row_ids = first_row + lax.broadcasted_iota(jnp.int32, (rows, cols), 0)
    col_ids = lax.broadcasted_iota(jnp.int32, (rows, cols), 1)
    chosen = []
    count = jnp.zeros((rows, cols), jnp.float32)
    for a in range(-HALF, HALF + 1):
        for b in range(-HALF, HALF + 1):
            inside = (row_ids + a >= 0) & (row_ids + a < total_rows)
            inside = inside & (col_ids + b >= 0) & (col_ids + b < cols)
            if (a, b) != (0, 0):
                inside = inside & (mask_ref[(a + HALF) * WIDTH + b + HALF] == 1)
            one = inside.astype(jnp.float32)
            chosen.append(one)
            count = count + one
    inverse = 1.0 / (count * ndate)

    def window(block):
        return max(0, block * LANE - SUB), min(cols, (block + 1) * LANE + SUB)

    coef[...] = jnp.zeros_like(coef)
    for block in range(blocks):
        begin, end = window(block)
        shape = (end - begin, LANE)
        shift = begin - block * LANE
        shift = shift + lax.broadcasted_iota(jnp.int32, shape, 0) - lax.broadcasted_iota(jnp.int32, shape, 1)
        for r in range(rows):
            for a in range(WIDTH):
                band = jnp.zeros(shape, jnp.float32)
                for b in range(WIDTH):
                    line = (chosen[a * WIDTH + b] * inverse)[r:r + 1, block * LANE:(block + 1) * LANE]
                    band = jnp.where(shift == b - HALF, line, band)
                weight[block, r, a, 0:end - begin, :] = band

    finish_power()
    power = jnp.sum(powers[...], axis=0)
    gain_row = lax.rsqrt(power * (1.0 / (total_rows * cols)) + 0.1)
    gain = jnp.broadcast_to(gain_row, (LANE, long_dates)).T[0:half_depth, :]
    gain = jnp.concatenate([gain] * blocks, axis=1)
    turned[...] = jnp.zeros_like(turned)

    def calibrate(source, place):
        for part in range(2):
            rows_here = slice(part * half_depth, (part + 1) * half_depth)
            scaled = (source[rows_here, :].astype(jnp.float32) * gain).astype(jnp.bfloat16)
            flat[rows_here, place * cols:(place + 1) * cols] = scaled
        turned[place] = flat[:, place * cols:(place + 1) * cols].T

    flat[...] = jnp.zeros_like(flat)
    for r in range(rows):
        calibrate(x_ref.at[r], r + HALF)

    @pl.when(has_prev)
    def _():
        up.wait_recv()

    @pl.when(has_next)
    def _():
        down.wait_recv()

    for r in range(HALF):
        calibrate(low.at[r], r)
        calibrate(high.at[r], r + HALF + rows)

    target = index_ref[0]
    picked = jnp.zeros((depth, LANE), jnp.float32)
    for r in range(rows):
        for block in range(blocks):
            begin, end = window(block)
            lanes = slice((r + HALF) * cols + block * LANE, (r + HALF) * cols + (block + 1) * LANE)
            real = flat[0:half_depth, lanes]
            imag = flat[half_depth:depth, lanes]
            for step in range(ITERS):
                pair = jnp.concatenate(
                    [jnp.concatenate([real, imag], axis=1), jnp.concatenate([imag, -real], axis=1)], axis=0
                )
                for a in range(WIDTH):
                    proj = jnp.dot(
                        turned[r + a, begin:end, 0:depth], pair, preferred_element_type=jnp.float32
                    )
                    band = weight[block, r, a, 0:end - begin, :]
                    both = jnp.concatenate([band, band], axis=1)
                    coef[block, a * cols + begin:a * cols + end, :] = (proj * both).astype(jnp.bfloat16)
                product = jnp.dot(
                    flat[0:depth, r * cols:(r + WIDTH) * cols], coef[block], preferred_element_type=jnp.float32
                )
                top, bottom = product[0:half_depth], product[half_depth:depth]
                new_real = top[:, 0:LANE] - bottom[:, LANE:2 * LANE]
                new_imag = top[:, LANE:2 * LANE] + bottom[:, 0:LANE]
                energy = jnp.sum(new_real * new_real + new_imag * new_imag, axis=0, keepdims=True)
                factor = lax.rsqrt(energy * (1.0 / ndate) + 0.001)
                new_real = new_real * factor
                new_imag = new_imag * factor
                real = new_real.astype(jnp.bfloat16)
                imag = new_imag.astype(jnp.bfloat16)
            lanes = slice(block * LANE, (block + 1) * LANE)
            out_ref[r, 0:half_depth, lanes] = new_real
            out_ref[r, half_depth:depth, lanes] = new_imag
            place = (first_row + r) * cols + block * LANE + lax.broadcasted_iota(jnp.int32, (1, LANE), 1)
            here = place == target
            picked = picked + jnp.concatenate(
                [jnp.where(here, new_real, 0.0), jnp.where(here, new_imag, 0.0)], axis=0
            )

    column[...] = jnp.zeros_like(column)
    column[0:depth, :] = picked
    refs[me] = row_of(column[...])
    start_ref()
    finish_ref()
    refvec = jnp.sum(refs[...], axis=0)
    refvec = jnp.broadcast_to(refvec, (LANE, long_depth)).T
    ref_real = refvec[0:half_depth]
    ref_imag = refvec[half_depth:depth]
    for r in range(rows):
        for block in range(blocks):
            lanes = slice(block * LANE, (block + 1) * LANE)
            real = out_ref[r, 0:half_depth, lanes]
            imag = out_ref[r, half_depth:depth, lanes]
            out_ref[r, 0:half_depth, lanes] = real * ref_real + imag * ref_imag
            out_ref[r, half_depth:depth, lanes] = imag * ref_real - real * ref_imag

    pl.when(has_next)(up.wait_send)
    pl.when(has_prev)(down.wait_send)


def per_device(slc, mask, ref_index):
    parts, ndate, rows, cols = slc.shape
    n = lax.axis_size("row")
    half_depth = round_up(ndate, SUB)
    depth = 2 * half_depth
    long_dates = round_up(half_depth, LANE)
    long_depth = round_up(depth, LANE)
    blocks = cols // LANE
    span = rows + 2 * HALF
    x = jnp.pad(slc.transpose(2, 0, 1, 3), ((0, 0), (0, 0), (0, half_depth - ndate), (0, 0)))
    x = x.reshape(rows, depth, cols)
    vmem = pl.BlockSpec(memory_space=pltpu.VMEM)

    def body(*refs):
        kernel(n, ndate, rows * n, *refs)

    out = pl.pallas_call(
        body,
        out_shape=jax.ShapeDtypeStruct((rows, depth, cols), jnp.float32),
        in_specs=[vmem, vmem, pl.BlockSpec(memory_space=pltpu.SMEM)],
        out_specs=vmem,
        scratch_shapes=[
            pltpu.VMEM((HALF, depth, cols), jnp.bfloat16),
            pltpu.VMEM((HALF, depth, cols), jnp.bfloat16),
            pltpu.VMEM((long_depth, span * cols), jnp.bfloat16),
            pltpu.VMEM((span, cols, long_depth), jnp.bfloat16),
            pltpu.VMEM((blocks, rows, WIDTH, LANE + 2 * SUB, LANE), jnp.float32),
            pltpu.VMEM((blocks, WIDTH * cols, 2 * LANE), jnp.bfloat16),
            pltpu.VMEM((long_depth, LANE), jnp.float32),
            pltpu.VMEM((n, 1, long_dates), jnp.float32),
            pltpu.VMEM((n, 1, long_depth), jnp.float32),
            pltpu.SemaphoreType.DMA((2,)),
            pltpu.SemaphoreType.DMA((2,)),
            pltpu.SemaphoreType.DMA((2, n)),
            pltpu.SemaphoreType.DMA((2, n)),
        ],
        compiler_params=pltpu.CompilerParams(collective_id=0, has_side_effects=True),
        name="link",
    )(x, mask, ref_index)
    out = out.reshape(rows, parts, half_depth, cols)[:, :, :ndate]
    return out.transpose(1, 2, 0, 3)


def solution(mesh):
    placed = (P(None, None, ("grp", "row"), None), P(None, ("grp", "row"), None), P("grp"))
    return jax.shard_map(
        per_device,
        mesh=mesh,
        in_specs=placed,
        out_specs=P(None, None, ("grp", "row"), None),
        check_vma=False,
    )
```

profile of v0, /device:TPU:0, one launch (start us, length us, event | category | flops | bytes accessed | tf_op | source)
XLA Modules:
  0.0 41.6 jit_solution(15884789283620566754)
XLA Ops:
  0.7 1.2 %copy.7 = bf16[2,2,300,256]{3,2,1,0:T(8,128)(2,1)S(1)} copy(bf16[2,2,300,256]{3,0,2,1:T(2,128)(2,1)} %bitcast.9) | data formatting | bytes 1228800
  1.8 0.9 %pad.4.clone = bf16[2,2,304,256]{3,2,1,0:T(8,128)(2,1)} pad(bf16[2,2,300,256]{3,2,1,0:T(8,128)(2,1)S(1)} %copy.7, bf16[]{:T(256)} %constant.2.clone.1), padding=0_0x0_0x0_4x0_0 | pad | bytes 1236994 | tf_op jit(solution)/shard_map/jit(_pad)/pad | solution.py:240
  2.7 35.6 %link.1 = f32[2,608,256]{2,1,0:T(8,128)} custom-call(bf16[2,608,256]{2,1,0:T(8,128)(2,1)} %bitcast.8, s32[25,2,256]{2,1,0:T(2,128)} %refs_1_.1, s32[1]{0:T(128)S(6)} %copy.10.refs_2_), custom_call_target="tpu_custom_call" | custom-call | tf_op jit(solution)/shard_map/link/pallas_call | solution.py:247
  38.3 3.3 %copy.9 = f32[2,2,300,256]{3,0,2,1:T(2,128)} copy(f32[2,2,300,256]{3,2,1,0:T(8,128)} %bitcast.7) | data formatting | bytes 2457600
where the time goes:
time: 41.8 us; the launch traced here: 41.6 us
  Pallas kernels  35.6 us (85%)
  local copies, waits for them, and re-layouts  5.3 us (13%)
  between operations  0.66 us (2%)
    pallas_call x1, Pallas kernels, per_device(): pl.pallas_call(body, out_shape=jax.ShapeDtypeStruct((rows, depth, cols),...  35.6 us
    unnamed x2, local copies, waits for them, and re-layouts  4.43 us
    pad x1, local copies, waits for them, and re-layouts, per_device(): jnp.pad(slc.transpose(2, 0, 1, 3), ((0, 0), (0, 0), (0, half_depth - ndat...  0.87 us

commit v1 on v0

--- a/solution.py
+++ b/solution.py
@@ -26,8 +26,9 @@
     low, high, flat, turned, weight, coef, column, powers, refs,
     low_sem, high_sem, power_sem, ref_sem,
 ):
-    rows, depth, cols = x_ref.shape
-    half_depth = depth // 2
+    rows, _, _, cols = x_ref.shape
+    half_depth = out_ref.shape[1] // 2
+    depth = 2 * half_depth
     blocks = cols // LANE
     long_dates = powers.shape[2]
     long_depth = refs.shape[2]
@@ -42,17 +43,6 @@
     @pl.loop(1, n)
     def _(k):
         pl.semaphore_signal(barrier, inc=1, device_id={"row": peer(k)}, device_id_type=MESH)
-
-    column[...] = jnp.zeros_like(column)
-    sums = jnp.zeros((half_depth, LANE), jnp.float32)
-    for r in range(rows):
-        for part in range(2):
-            for block in range(blocks):
-                piece = x_ref[r, part * half_depth:(part + 1) * half_depth, block * LANE:(block + 1) * LANE]
-                piece = piece.astype(jnp.float32)
-                sums = sums + piece * piece
-    column[0:half_depth, :] = sums
-    powers[me] = row_of(column[0:long_dates, :])
 
     pl.semaphore_wait(barrier, n - 1)
 
@@ -82,7 +72,6 @@
 
     start_power, finish_power = exchange(powers, power_sem)
     start_ref, finish_ref = exchange(refs, ref_sem)
-    start_power()
 
     up = pltpu.make_async_remote_copy(
         src_ref=x_ref.at[rows - HALF:rows], dst_ref=low, send_sem=low_sem.at[0], recv_sem=low_sem.at[1],
@@ -96,6 +85,19 @@
     has_prev = me > 0
     pl.when(has_next)(up.start)
     pl.when(has_prev)(down.start)
+
+    column[...] = jnp.zeros_like(column)
+    sums = jnp.zeros((ndate, LANE), jnp.float32)
+    for r in range(rows):
+        for part in range(2):
+            for block in range(blocks):
+                piece = x_ref[r, part, :, block * LANE:(block + 1) * LANE]
+                piece = piece.astype(jnp.float32)
+                sums = sums + piece * piece
+    column[0:ndate, :] = sums
+    powers[me] = row_of(column[0:long_dates, :])
+
+    start_power()
 
     @pl.when(me == 0)
     def _():
@@ -140,14 +142,14 @@
     finish_power()
     power = jnp.sum(powers[...], axis=0)
     gain_row = lax.rsqrt(power * (1.0 / (total_rows * cols)) + 0.1)
-    gain = jnp.broadcast_to(gain_row, (LANE, long_dates)).T[0:half_depth, :]
+    gain = jnp.broadcast_to(gain_row, (LANE, long_dates)).T[0:ndate, :]
     gain = jnp.concatenate([gain] * blocks, axis=1)
     turned[...] = jnp.zeros_like(turned)
 
     def calibrate(source, place):
         for part in range(2):
-            rows_here = slice(part * half_depth, (part + 1) * half_depth)
-            scaled = (source[rows_here, :].astype(jnp.float32) * gain).astype(jnp.bfloat16)
+            rows_here = slice(part * half_depth, part * half_depth + ndate)
+            scaled = (source[part].astype(jnp.float32) * gain).astype(jnp.bfloat16)
             flat[rows_here, place * cols:(place + 1) * cols] = scaled
         turned[place] = flat[:, place * cols:(place + 1) * cols].T
 
@@ -237,8 +239,7 @@
     long_depth = round_up(depth, LANE)
     blocks = cols // LANE
     span = rows + 2 * HALF
-    x = jnp.pad(slc.transpose(2, 0, 1, 3), ((0, 0), (0, 0), (0, half_depth - ndate), (0, 0)))
-    x = x.reshape(rows, depth, cols)
+    x = slc.transpose(2, 0, 1, 3)
     vmem = pl.BlockSpec(memory_space=pltpu.VMEM)
 
     def body(*refs):
@@ -250,8 +251,8 @@
         in_specs=[vmem, vmem, pl.BlockSpec(memory_space=pltpu.SMEM)],
         out_specs=vmem,
         scratch_shapes=[
-            pltpu.VMEM((HALF, depth, cols), jnp.bfloat16),
-            pltpu.VMEM((HALF, depth, cols), jnp.bfloat16),
+            pltpu.VMEM((HALF, parts, ndate, cols), jnp.bfloat16),
+            pltpu.VMEM((HALF, parts, ndate, cols), jnp.bfloat16),
             pltpu.VMEM((long_depth, span * cols), jnp.bfloat16),
             pltpu.VMEM((span, cols, long_depth), jnp.bfloat16),
             pltpu.VMEM((blocks, rows, WIDTH, LANE + 2 * SUB, LANE), jnp.float32),

time: 41.8 us -> 42.4 us (1.014)
  Pallas kernels: 35.6 us -> 36.2 us
    pad x1 -> x0, local copies, waits for them, and re-layouts: 0.87 us -> none  [per_device(): jnp.pad(slc.transpose(2, 0, 1, 3), ((0, 0), (0, 0), (0, half_depth - ndat...]
    unnamed x2, local copies, waits for them, and re-layouts: 4.43 us -> 5.26 us
    pallas_call x1, Pallas kernels: 35.6 us -> 36.2 us  [per_device(): pl.pallas_call(body, out_shape=jax.ShapeDtypeStruct((rows, depth, cols),...]
where the time goes in v1:
time: 42.4 us; the launch traced here: 42.2 us
  Pallas kernels  36.2 us (85%)
  local copies, waits for them, and re-layouts  5.26 us (12%)
  between operations  0.66 us (2%)
    pallas_call x1, Pallas kernels, per_device(): pl.pallas_call(body, out_shape=jax.ShapeDtypeStruct((rows, depth, cols),...  36.2 us
    unnamed x2, local copies, waits for them, and re-layouts  5.26 us

profile of v1, /device:TPU:0, one launch (start us, length us, event | category | flops | bytes accessed | tf_op | source)
XLA Modules:
  0.0 42.2 jit_solution(17153950385092522230)
XLA Ops:
  0.7 2.0 %copy.10 = bf16[2,300,2,256]{3,1,0,2:T(8,128)(2,1)} copy(bf16[2,300,2,256]{3,2,1,0:T(2,128)(2,1)} %param.3) | data formatting | bytes 1228800 | tf_op args[0]
  2.6 36.2 %link.1 = f32[2,608,256]{2,1,0:T(8,128)} custom-call(bf16[2,2,300,256]{3,2,1,0:T(8,128)(2,1)} %bitcast.9, s32[25,2,256]{2,1,0:T(2,128)} %refs_1_.1, s32[1]{0:T(128)S(6)} %copy.11.refs_2_), custom_call_target="tpu_custom_call" | custom-call | tf_op jit(solution)/shard_map/link/pallas_call | solution.py:248
  38.9 3.3 %copy.9 = f32[2,2,300,256]{3,0,2,1:T(2,128)} copy(f32[2,2,300,256]{3,2,1,0:T(8,128)} %bitcast.8) | data formatting | bytes 2457600

commit v2 on v0

--- a/solution.py
+++ b/solution.py
@@ -23,7 +23,7 @@
 
 def kernel(
     n, ndate, total_rows, x_ref, mask_ref, index_ref, out_ref,
-    low, high, flat, turned, weight, coef, column, powers, refs,
+    low, high, flat, turned, weight, coef, total, column, powers, refs,
     low_sem, high_sem, power_sem, ref_sem,
 ):
     rows, depth, cols = x_ref.shape
@@ -84,18 +84,25 @@
     start_ref, finish_ref = exchange(refs, ref_sem)
     start_power()
 
-    up = pltpu.make_async_remote_copy(
-        src_ref=x_ref.at[rows - HALF:rows], dst_ref=low, send_sem=low_sem.at[0], recv_sem=low_sem.at[1],
-        device_id={"row": jnp.minimum(me + 1, n - 1)}, device_id_type=MESH,
-    )
-    down = pltpu.make_async_remote_copy(
-        src_ref=x_ref.at[0:HALF], dst_ref=high, send_sem=high_sem.at[0], recv_sem=high_sem.at[1],
-        device_id={"row": jnp.maximum(me - 1, 0)}, device_id_type=MESH,
-    )
+    def halo(t):
+        up = pltpu.make_async_remote_copy(
+            src_ref=x_ref.at[rows - t], dst_ref=low.at[HALF - t],
+            send_sem=low_sem.at[0, t - 1], recv_sem=low_sem.at[1, t - 1],
+            device_id={"row": jnp.minimum(me + 1, n - 1)}, device_id_type=MESH,
+        )
+        down = pltpu.make_async_remote_copy(
+            src_ref=x_ref.at[t - 1], dst_ref=high.at[t - 1],
+            send_sem=high_sem.at[0, t - 1], recv_sem=high_sem.at[1, t - 1],
+            device_id={"row": jnp.maximum(me - 1, 0)}, device_id_type=MESH,
+        )
+        return up, down
+
     has_next = me < n - 1
     has_prev = me > 0
-    pl.when(has_next)(up.start)
-    pl.when(has_prev)(down.start)
+    for t in range(1, HALF + 1):
+        up, down = halo(t)
+        pl.when(has_next)(up.start)
+        pl.when(has_prev)(down.start)
 
     @pl.when(me == 0)
     def _():
@@ -152,43 +159,81 @@
         turned[place] = flat[:, place * cols:(place + 1) * cols].T
 
     flat[...] = jnp.zeros_like(flat)
+    def tile(r, block):
+        start = (r + HALF) * cols + block * LANE
+        return flat[0:half_depth, start:start + LANE], flat[half_depth:depth, start:start + LANE]
+
+    def pair_of(real, imag):
+        return jnp.concatenate(
+            [jnp.concatenate([real, imag], axis=1), jnp.concatenate([imag, -real], axis=1)], axis=0
+        )
+
+    def project(r, block, a, pair):
+        begin, end = window(block)
+        proj = jnp.dot(turned[r + a, begin:end, 0:depth], pair, preferred_element_type=jnp.float32)
+        band = weight[block, r, a, 0:end - begin, :]
+        both = jnp.concatenate([band, band], axis=1)
+        coef[block, a * cols + begin:a * cols + end, :] = (proj * both).astype(jnp.bfloat16)
+
+    def update(r, block, first, last):
+        return jnp.dot(
+            flat[0:depth, (r + first) * cols:(r + last) * cols],
+            coef[block, first * cols:last * cols, :], preferred_element_type=jnp.float32,
+        )
+
+    def partial_update(r, block, places):
+        pair = pair_of(*tile(r, block))
+        value = None
+        for low_place, high_place in places:
+            first, last = max(low_place - r, 0), min(high_place - r, WIDTH)
+            if first >= last:
+                continue
+            for a in range(first, last):
+                project(r, block, a, pair)
+            term = update(r, block, first, last)
+            value = term if value is None else value + term
+        return value
+
     for r in range(rows):
         calibrate(x_ref.at[r], r + HALF)
-
-    @pl.when(has_prev)
-    def _():
-        up.wait_recv()
-
-    @pl.when(has_next)
-    def _():
-        down.wait_recv()
-
-    for r in range(HALF):
-        calibrate(low.at[r], r)
-        calibrate(high.at[r], r + HALF + rows)
+    for r in range(rows):
+        for block in range(blocks):
+            total[r, block] = partial_update(r, block, [(HALF, HALF + rows)])
+
+    def arrive(t):
+        up, down = halo(t)
+        pl.when(has_prev)(up.wait_recv)
+        pl.when(has_next)(down.wait_recv)
+        calibrate(low.at[HALF - t], HALF - t)
+        calibrate(high.at[t - 1], HALF + rows + t - 1)
+
+    def ring(t):
+        return [(HALF - t, HALF - t + 1), (HALF + rows + t - 1, HALF + rows + t)]
+
+    for t in range(1, HALF):
+        arrive(t)
+        for r in range(rows):
+            for block in range(blocks):
+                term = partial_update(r, block, ring(t))
+                if term is not None:
+                    total[r, block] += term
+    arrive(HALF)
 
     target = index_ref[0]
     picked = jnp.zeros((depth, LANE), jnp.float32)
     for r in range(rows):
         for block in range(blocks):
-            begin, end = window(block)
-            lanes = slice((r + HALF) * cols + block * LANE, (r + HALF) * cols + (block + 1) * LANE)
-            real = flat[0:half_depth, lanes]
-            imag = flat[half_depth:depth, lanes]
             for step in range(ITERS):
-                pair = jnp.concatenate(
-                    [jnp.concatenate([real, imag], axis=1), jnp.concatenate([imag, -real], axis=1)], axis=0
-                )
-                for a in range(WIDTH):
-                    proj = jnp.dot(
-                        turned[r + a, begin:end, 0:depth], pair, preferred_element_type=jnp.float32
-                    )
-                    band = weight[block, r, a, 0:end - begin, :]
-                    both = jnp.concatenate([band, band], axis=1)
-                    coef[block, a * cols + begin:a * cols + end, :] = (proj * both).astype(jnp.bfloat16)
-                product = jnp.dot(
-                    flat[0:depth, r * cols:(r + WIDTH) * cols], coef[block], preferred_element_type=jnp.float32
-                )
+                if step == 0:
+                    product = total[r, block]
+                    term = partial_update(r, block, ring(HALF))
+                    if term is not None:
+                        product = product + term
+                else:
+                    pair = pair_of(real, imag)
+                    for a in range(WIDTH):
+                        project(r, block, a, pair)
+                    product = update(r, block, 0, WIDTH)
                 top, bottom = product[0:half_depth], product[half_depth:depth]
                 new_real = top[:, 0:LANE] - bottom[:, LANE:2 * LANE]
                 new_imag = top[:, LANE:2 * LANE] + bottom[:, 0:LANE]
@@ -224,8 +269,10 @@
             out_ref[r, 0:half_depth, lanes] = real * ref_real + imag * ref_imag
             out_ref[r, half_depth:depth, lanes] = imag * ref_real - real * ref_imag
 
-    pl.when(has_next)(up.wait_send)
-    pl.when(has_prev)(down.wait_send)
+    for t in range(1, HALF + 1):
+        up, down = halo(t)
+        pl.when(has_next)(up.wait_send)
+        pl.when(has_prev)(down.wait_send)
 
 
 def per_device(slc, mask, ref_index):
@@ -256,11 +303,12 @@
             pltpu.VMEM((span, cols, long_depth), jnp.bfloat16),
             pltpu.VMEM((blocks, rows, WIDTH, LANE + 2 * SUB, LANE), jnp.float32),
             pltpu.VMEM((blocks, WIDTH * cols, 2 * LANE), jnp.bfloat16),
+            pltpu.VMEM((rows, blocks, depth, 2 * LANE), jnp.float32),
             pltpu.VMEM((long_depth, LANE), jnp.float32),
             pltpu.VMEM((n, 1, long_dates), jnp.float32),
             pltpu.VMEM((n, 1, long_depth), jnp.float32),
-            pltpu.SemaphoreType.DMA((2,)),
-            pltpu.SemaphoreType.DMA((2,)),
+            pltpu.SemaphoreType.DMA((2, HALF)),
+            pltpu.SemaphoreType.DMA((2, HALF)),
             pltpu.SemaphoreType.DMA((2, n)),
             pltpu.SemaphoreType.DMA((2, n)),
         ],

time: 41.8 us -> 40.2 us (0.962)
  Pallas kernels: 35.6 us -> 34.1 us
    pallas_call x1, Pallas kernels: 35.6 us -> 34.1 us  [per_device(): pl.pallas_call(body, out_shape=jax.ShapeDtypeStruct((rows, depth, cols),...]
where the time goes in v2:
time: 40.2 us; the launch traced here: 40 us
  Pallas kernels  34.1 us (85%)
  local copies, waits for them, and re-layouts  5.3 us (13%)
  between operations  0.66 us (2%)
    pallas_call x1, Pallas kernels, per_device(): pl.pallas_call(body, out_shape=jax.ShapeDtypeStruct((rows, depth, cols),...  34.1 us
    unnamed x2, local copies, waits for them, and re-layouts  4.43 us
    pad x1, local copies, waits for them, and re-layouts, per_device(): jnp.pad(slc.transpose(2, 0, 1, 3), ((0, 0), (0, 0), (0, half_depth - ndat...  0.87 us

profile of v2, /device:TPU:0, one launch (start us, length us, event | category | flops | bytes accessed | tf_op | source)
XLA Modules:
  0.0 40.0 jit_solution(1650810643809668912)
XLA Ops:
  0.7 1.2 %copy.7 = bf16[2,2,300,256]{3,2,1,0:T(8,128)(2,1)S(1)} copy(bf16[2,2,300,256]{3,0,2,1:T(2,128)(2,1)} %bitcast.9) | data formatting | bytes 1228800
  1.8 0.9 %pad.4.clone = bf16[2,2,304,256]{3,2,1,0:T(8,128)(2,1)} pad(bf16[2,2,300,256]{3,2,1,0:T(8,128)(2,1)S(1)} %copy.7, bf16[]{:T(256)} %constant.2.clone.1), padding=0_0x0_0x0_4x0_0 | pad | bytes 1236994 | tf_op jit(solution)/shard_map/jit(_pad)/pad | solution.py:287
  2.7 34.1 %link.1 = f32[2,608,256]{2,1,0:T(8,128)} custom-call(bf16[2,608,256]{2,1,0:T(8,128)(2,1)} %bitcast.8, s32[25,2,256]{2,1,0:T(2,128)} %refs_1_.1, s32[1]{0:T(128)S(6)} %copy.10.refs_2_), custom_call_target="tpu_custom_call" | custom-call | tf_op jit(solution)/shard_map/link/pallas_call | solution.py:294
  36.8 3.3 %copy.9 = f32[2,2,300,256]{3,0,2,1:T(2,128)} copy(f32[2,2,300,256]{3,2,1,0:T(8,128)} %bitcast.7) | data formatting | bytes 2457600

commit v3 on v2

--- a/solution.py
+++ b/solution.py
@@ -144,12 +144,12 @@
                     band = jnp.where(shift == b - HALF, line, band)
                 weight[block, r, a, 0:end - begin, :] = band
 
+    flat[depth:, :] = jnp.zeros((flat.shape[0] - depth, flat.shape[1]), flat.dtype)
     finish_power()
     power = jnp.sum(powers[...], axis=0)
     gain_row = lax.rsqrt(power * (1.0 / (total_rows * cols)) + 0.1)
     gain = jnp.broadcast_to(gain_row, (LANE, long_dates)).T[0:half_depth, :]
     gain = jnp.concatenate([gain] * blocks, axis=1)
-    turned[...] = jnp.zeros_like(turned)
 
     def calibrate(source, place):
         for part in range(2):
@@ -158,7 +158,6 @@
             flat[rows_here, place * cols:(place + 1) * cols] = scaled
         turned[place] = flat[:, place * cols:(place + 1) * cols].T
 
-    flat[...] = jnp.zeros_like(flat)
     def tile(r, block):
         start = (r + HALF) * cols + block * LANE
         return flat[0:half_depth, start:start + LANE], flat[half_depth:depth, start:start + LANE]
@@ -168,12 +167,16 @@
             [jnp.concatenate([real, imag], axis=1), jnp.concatenate([imag, -real], axis=1)], axis=0
         )
 
-    def project(r, block, a, pair):
+    def project(r, block, first, last, pair):
         begin, end = window(block)
-        proj = jnp.dot(turned[r + a, begin:end, 0:depth], pair, preferred_element_type=jnp.float32)
-        band = weight[block, r, a, 0:end - begin, :]
-        both = jnp.concatenate([band, band], axis=1)
-        coef[block, a * cols + begin:a * cols + end, :] = (proj * both).astype(jnp.bfloat16)
+        size = end - begin
+        near = turned[r + first:r + last, begin:end, 0:depth].reshape((last - first) * size, depth)
+        proj = jnp.dot(near, pair, preferred_element_type=jnp.float32)
+        for a in range(first, last):
+            band = weight[block, r, a, 0:size, :]
+            both = jnp.concatenate([band, band], axis=1)
+            piece = proj[(a - first) * size:(a - first + 1) * size]
+            coef[block, a * cols + begin:a * cols + end, :] = (piece * both).astype(jnp.bfloat16)
 
     def update(r, block, first, last):
         return jnp.dot(
@@ -188,8 +191,7 @@
             first, last = max(low_place - r, 0), min(high_place - r, WIDTH)
             if first >= last:
                 continue
-            for a in range(first, last):
-                project(r, block, a, pair)
+            project(r, block, first, last, pair)
             term = update(r, block, first, last)
             value = term if value is None else value + term
         return value
@@ -231,8 +233,7 @@
                         product = product + term
                 else:
                     pair = pair_of(real, imag)
-                    for a in range(WIDTH):
-                        project(r, block, a, pair)
+                    project(r, block, 0, WIDTH, pair)
                     product = update(r, block, 0, WIDTH)
                 top, bottom = product[0:half_depth], product[half_depth:depth]
                 new_real = top[:, 0:LANE] - bottom[:, LANE:2 * LANE]

time: 40.2 us -> 41.1 us (1.022)
  Pallas kernels: 34.1 us -> 34.9 us
    pallas_call x1, Pallas kernels: 34.1 us -> 34.9 us  [per_device(): pl.pallas_call(body, out_shape=jax.ShapeDtypeStruct((rows, depth, cols),...]
where the time goes in v3:
time: 41.1 us; the launch traced here: 40.9 us
  Pallas kernels  34.9 us (85%)
  local copies, waits for them, and re-layouts  5.3 us (13%)
  between operations  0.66 us (2%)
    pallas_call x1, Pallas kernels, per_device(): pl.pallas_call(body, out_shape=jax.ShapeDtypeStruct((rows, depth, cols),...  34.9 us
    unnamed x2, local copies, waits for them, and re-layouts  4.43 us
    pad x1, local copies, waits for them, and re-layouts, per_device(): jnp.pad(slc.transpose(2, 0, 1, 3), ((0, 0), (0, 0), (0, half_depth - ndat...  0.87 us

profile of v3, /device:TPU:0, one launch (start us, length us, event | category | flops | bytes accessed | tf_op | source)
XLA Modules:
  0.0 40.9 jit_solution(6925885175771970541)
XLA Ops:
  0.7 1.2 %copy.7 = bf16[2,2,300,256]{3,2,1,0:T(8,128)(2,1)S(1)} copy(bf16[2,2,300,256]{3,0,2,1:T(2,128)(2,1)} %bitcast.9) | data formatting | bytes 1228800
  1.8 0.9 %pad.4.clone = bf16[2,2,304,256]{3,2,1,0:T(8,128)(2,1)} pad(bf16[2,2,300,256]{3,2,1,0:T(8,128)(2,1)S(1)} %copy.7, bf16[]{:T(256)} %constant.2.clone.1), padding=0_0x0_0x0_4x0_0 | pad | bytes 1236994 | tf_op jit(solution)/shard_map/jit(_pad)/pad | solution.py:288
  2.7 34.9 %link.1 = f32[2,608,256]{2,1,0:T(8,128)} custom-call(bf16[2,608,256]{2,1,0:T(8,128)(2,1)} %bitcast.8, s32[25,2,256]{2,1,0:T(2,128)} %refs_1_.1, s32[1]{0:T(128)S(6)} %copy.10.refs_2_), custom_call_target="tpu_custom_call" | custom-call | tf_op jit(solution)/shard_map/link/pallas_call | solution.py:295
  37.6 3.3 %copy.9 = f32[2,2,300,256]{3,0,2,1:T(2,128)} copy(f32[2,2,300,256]{3,2,1,0:T(8,128)} %bitcast.7) | data formatting | bytes 2457600

commit v4 on v2

--- a/solution.py
+++ b/solution.py
@@ -144,12 +144,12 @@
                     band = jnp.where(shift == b - HALF, line, band)
                 weight[block, r, a, 0:end - begin, :] = band
 
+    flat[depth:, :] = jnp.zeros((flat.shape[0] - depth, flat.shape[1]), flat.dtype)
     finish_power()
     power = jnp.sum(powers[...], axis=0)
     gain_row = lax.rsqrt(power * (1.0 / (total_rows * cols)) + 0.1)
     gain = jnp.broadcast_to(gain_row, (LANE, long_dates)).T[0:half_depth, :]
     gain = jnp.concatenate([gain] * blocks, axis=1)
-    turned[...] = jnp.zeros_like(turned)
 
     def calibrate(source, place):
         for part in range(2):
@@ -158,7 +158,6 @@
             flat[rows_here, place * cols:(place + 1) * cols] = scaled
         turned[place] = flat[:, place * cols:(place + 1) * cols].T
 
-    flat[...] = jnp.zeros_like(flat)
     def tile(r, block):
         start = (r + HALF) * cols + block * LANE
         return flat[0:half_depth, start:start + LANE], flat[half_depth:depth, start:start + LANE]

time: 40.2 us -> 40.2 us (level)
  no operation moved by 1% of the time
where the time goes in v4:
time: 40.2 us; the launch traced here: 40 us
  Pallas kernels  34.1 us (85%)
  local copies, waits for them, and re-layouts  5.3 us (13%)
  between operations  0.66 us (2%)
    pallas_call x1, Pallas kernels, per_device(): pl.pallas_call(body, out_shape=jax.ShapeDtypeStruct((rows, depth, cols),...  34.1 us
    unnamed x2, local copies, waits for them, and re-layouts  4.43 us
    pad x1, local copies, waits for them, and re-layouts, per_device(): jnp.pad(slc.transpose(2, 0, 1, 3), ((0, 0), (0, 0), (0, half_depth - ndat...  0.87 us

profile of v4, /device:TPU:0, one launch (start us, length us, event | category | flops | bytes accessed | tf_op | source)
XLA Modules:
  0.0 40.0 jit_solution(14058616734155254170)
XLA Ops:
  0.7 1.2 %copy.7 = bf16[2,2,300,256]{3,2,1,0:T(8,128)(2,1)S(1)} copy(bf16[2,2,300,256]{3,0,2,1:T(2,128)(2,1)} %bitcast.9) | data formatting | bytes 1228800
  1.8 0.9 %pad.4.clone = bf16[2,2,304,256]{3,2,1,0:T(8,128)(2,1)} pad(bf16[2,2,300,256]{3,2,1,0:T(8,128)(2,1)S(1)} %copy.7, bf16[]{:T(256)} %constant.2.clone.1), padding=0_0x0_0x0_4x0_0 | pad | bytes 1236994 | tf_op jit(solution)/shard_map/jit(_pad)/pad | solution.py:286
  2.7 34.1 %link.1 = f32[2,608,256]{2,1,0:T(8,128)} custom-call(bf16[2,608,256]{2,1,0:T(8,128)(2,1)} %bitcast.8, s32[25,2,256]{2,1,0:T(2,128)} %refs_1_.1, s32[1]{0:T(128)S(6)} %copy.10.refs_2_), custom_call_target="tpu_custom_call" | custom-call | tf_op jit(solution)/shard_map/link/pallas_call | solution.py:293
  36.8 3.3 %copy.9 = f32[2,2,300,256]{3,0,2,1:T(2,128)} copy(f32[2,2,300,256]{3,2,1,0:T(8,128)} %bitcast.7) | data formatting | bytes 2457600
